TPU v7x, 32 devices: a whole 2x2x4 slice. The times are simulated.
32 devices in a mesh: fsdp: 16 (over z, y, core), tp: 2 (over x).
Axes of the slice: x: 2, y: 2, z: 4, core: 2. Of those that a mesh axis runs over, the one named last changes fastest.
Arguments:
- tokens: bfloat16 [16, 1024, 1152], P('fsdp', 'tp'), may hold values from -6 to 6
- condition: bfloat16 [16, 1152], P('fsdp'), may hold values from -3 to 3
- mod_weight: bfloat16 [1152, 6912], P('tp', 'fsdp'), may hold values from -0.088388348 to 0.088388348
- mod_bias: bfloat16 [6912], P('fsdp'), may hold values from -1.5 to 1.5
- qkv_weight: bfloat16 [1152, 3, 1152], P('fsdp', None, 'tp'), may hold values from -0.088388348 to 0.088388348
- qv_bias: bfloat16 [2, 1152], P(None, 'fsdp'), may hold values from -2 to 2
- out_weight: bfloat16 [1152, 1152], P('tp', 'fsdp'), may hold values from -0.75 to 0.75
- out_bias: bfloat16 [1152], P('fsdp'), may hold values from -3 to 3
- up_weight: bfloat16 [1152, 4608], P('fsdp', 'tp'), may hold values from -0.1875 to 0.1875
- up_bias: bfloat16 [4608], P('fsdp'), may hold values from -3 to 3
- down_weight: bfloat16 [4608, 1152], P('tp', 'fsdp'), may hold values from -0.09375 to 0.09375
- down_bias: bfloat16 [1152], P('fsdp'), may hold values from -3 to 3
- cotangent: bfloat16 [16, 1024, 1152], P('fsdp', 'tp'), may hold values from -6 to 6
Outputs:
- result: bfloat16 [16, 1024, 1152], P('fsdp', 'tp')
- tokens_grad: bfloat16 [16, 1024, 1152], P('fsdp', 'tp')
- condition_grad: float32 [16, 1152], P('fsdp', 'tp')
- mod_weight_grad: float32 [1152, 6912], P('tp', 'fsdp')
- mod_bias_grad: float32 [6912], P('fsdp')
- qkv_weight_grad: float32 [1152, 3, 1152], P('fsdp', None, 'tp')
- qv_bias_grad: float32 [2, 1152], P(None, 'fsdp')
- out_weight_grad: float32 [1152, 1152], P('tp', 'fsdp')
- out_bias_grad: float32 [1152], P('fsdp')
- up_weight_grad: float32 [1152, 4608], P('fsdp', 'tp')
- up_bias_grad: float32 [4608], P('fsdp')
- down_weight_grad: float32 [4608, 1152], P('tp', 'fsdp')
- down_bias_grad: float32 [1152], P('fsdp')
All inputs are finite; a program needn't handle non-finite values.
Results may differ from a plain program's by a relative error of at most 0.015.
Values may be sent and summed in bfloat16 or wider, within the bound.
A program may use at most 256 MiB of HBM per device.

v0:
```python
import math
import jax
import jax.numpy as jnp
from jax import lax
from jax.sharding import PartitionSpec as P

HEAD_DIM = 72
EPSILON = 1e-06
HIGH = lax.Precision.HIGHEST


def normalize(values):
    center = values - jnp.mean(values, axis=-1, keepdims=True)
    variance = jnp.mean(center * center, axis=-1, keepdims=True)
    inverse = lax.rsqrt(variance + EPSILON)
    return (center * inverse, inverse)


def norm_back(grad_norm, normed, inverse):
    first_mean = jnp.mean(grad_norm, axis=-1, keepdims=True)
    second_mean = jnp.mean(grad_norm * normed, axis=-1, keepdims=True)
    return inverse * (grad_norm - first_mean - normed * second_mean)


def inner_rows(left, right):
    return lax.dot_general(
        left, right, (((0,), (0,)), ((), ())), preferred_element_type=jnp.float32
    )


def outer_cols(left, right):
    return lax.dot_general(
        left, right, (((1,), (1,)), ((), ())), preferred_element_type=jnp.float32
    )


def gelu_tanh(values):
    return jax.nn.gelu(values, approximate=True)


def to_heads(flat, head_count):
    return flat.reshape(flat.shape[0], head_count, HEAD_DIM).transpose(1, 0, 2)


def from_heads(stacked):
    return stacked.transpose(1, 0, 2).reshape(stacked.shape[1], stacked.shape[0] * HEAD_DIM)


def swap(values):
    return lax.ppermute(values, "tp", [(0, 1), (1, 0)])


def gather_rows(values, tp_count):
    if tp_count == 2:
        return jnp.concatenate([values, swap(values)], axis=0)
    return lax.all_gather(values, "tp", axis=0, tiled=True)


def scatter_rows(left, right, contract, tp_count):
    if tp_count == 2:
        half = left.shape[0] // 2
        sent = swap(contract(left[half:], right).astype(jnp.bfloat16))
        return contract(left[:half], right) + sent.astype(jnp.float32)
    return lax.psum_scatter(
        contract(left, right).astype(jnp.bfloat16), "tp", scatter_dimension=0, tiled=True
    ).astype(jnp.float32)


def sum_pair(values, tp_count):
    if tp_count == 2:
        return values + swap(values)
    return lax.psum(values, "tp")


def plain(left, right):
    return jnp.dot(left, right, preferred_element_type=jnp.float32)


def reduce_grad(term, axis):
    return lax.psum_scatter(term.astype(jnp.bfloat16), "fsdp", scatter_dimension=axis, tiled=True)


def gather_small(flat):
    size = flat.shape[0]
    padded = -(-size // 1024) * 1024
    block = jnp.pad(flat, (0, padded - size)).reshape(8, padded // 8)
    return lax.all_gather(block, "fsdp", axis=0, tiled=True).reshape(-1, padded)[:, :size]


def trade(rows):
    return lax.all_to_all(rows, "fsdp", split_axis=0, concat_axis=0, tiled=True)


def shards(
    tokens,
    condition,
    mod_weight,
    mod_bias,
    qkv_weight,
    qv_bias,
    out_weight,
    out_bias,
    up_weight,
    up_bias,
    down_weight,
    down_bias,
    cotangent,
):
    tp_count = lax.axis_size("tp")
    tp_place = lax.axis_index("tp")
    fsdp_count = lax.axis_size("fsdp")
    local_rows = tokens.shape[1]
    width = tokens.shape[2]
    seq_len = local_rows * tp_count
    share = width // tp_count
    thin = width // fsdp_count
    hidden_thin = up_bias.shape[0]
    hidden_full = hidden_thin * fsdp_count
    mod_thin = mod_bias.shape[0]
    small = gather_small(
        jnp.concatenate([condition[0], qv_bias.reshape(-1), out_bias, up_bias, down_bias])
    ).astype(jnp.float32)
    qkv_full = lax.all_gather(qkv_weight, "fsdp", axis=0, tiled=True)
    out_full = lax.all_gather(out_weight, "fsdp", axis=1, tiled=True)
    up_full = lax.all_gather(up_weight, "fsdp", axis=0, tiled=True)
    down_full = lax.all_gather(down_weight, "fsdp", axis=1, tiled=True)
    cond_all = small[:, :width]
    spot = width
    qv_full = (
        small[:, spot : spot + 2 * thin]
        .reshape(fsdp_count, 2, thin)
        .transpose(1, 0, 2)
        .reshape(2, width)
    )
    spot += 2 * thin
    out_shift = small[:, spot : spot + thin].reshape(-1)
    spot += thin
    up_shift = small[:, spot : spot + hidden_thin].reshape(-1)
    spot += hidden_thin
    down_shift = small[:, spot : spot + thin].reshape(-1)
    head_cols = qkv_full.shape[2]
    head_count = head_cols // HEAD_DIM
    hidden_cols = up_full.shape[1]
    cond_part = lax.dynamic_slice_in_dim(cond_all, tp_place * share, share, 1)
    silu_low = jax.nn.silu(cond_part).astype(jnp.bfloat16)
    partial_mod = jnp.dot(silu_low, mod_weight, preferred_element_type=jnp.float32)
    modulation = trade(sum_pair(partial_mod, tp_count) + mod_bias.astype(jnp.float32)).reshape(-1)
    pieces = modulation.reshape(6, width)
    shift_one = pieces[0]
    scale_one = pieces[1]
    gate_one = pieces[2]
    shift_two = pieces[3]
    scale_two = pieces[4]
    gate_two = pieces[5]
    rows_in = tokens[0].astype(jnp.float32)
    normed_one, inverse_one = normalize(rows_in)
    hidden_one = gather_rows(
        (normed_one * (1.0 + scale_one) + shift_one).astype(jnp.bfloat16), tp_count
    )
    qkv_matrix = qkv_full.reshape(width, 3 * head_cols)
    projected = plain(hidden_one, qkv_matrix).reshape(seq_len, 3, head_cols)
    qv_local = lax.dynamic_slice_in_dim(qv_full, tp_place * head_cols, head_cols, 1)
    queries = to_heads((projected[:, 0] + qv_local[0]).astype(jnp.bfloat16), head_count)
    keys_all = to_heads(projected[:, 1].astype(jnp.bfloat16), head_count)
    values_all = to_heads((projected[:, 2] + qv_local[1]).astype(jnp.bfloat16), head_count)
    grad_rows = cotangent[0].astype(jnp.float32)
    grad_two_own = (grad_rows * gate_two).astype(jnp.bfloat16)
    grad_branch_two = gather_rows(grad_two_own, tp_count)
    block = min(512, seq_len)
    block_count = seq_len // block
    scaling = 1.0 / math.sqrt(HEAD_DIM)
    query_blocks = queries.reshape(head_count, block_count, block, HEAD_DIM).transpose(1, 0, 2, 3)

    def attend(query_block):
        scores = (
            jnp.einsum("hqd,hkd->hqk", query_block, keys_all, preferred_element_type=jnp.float32)
            * scaling
        )
        highest = jnp.max(scores, axis=-1, keepdims=True)
        raised = jnp.exp(scores - highest)
        totals = jnp.sum(raised, axis=-1, keepdims=True)
        weights = (raised / totals).astype(jnp.bfloat16)
        output = jnp.einsum("hqk,hkd->hqd", weights, values_all, preferred_element_type=jnp.float32)
        return (output, (highest + jnp.log(totals))[..., 0])

    attended_blocks, log_totals = lax.map(attend, query_blocks)
    attended = attended_blocks.transpose(1, 0, 2, 3).reshape(head_count, seq_len, HEAD_DIM)
    attended_low = from_heads(attended).astype(jnp.bfloat16)
    branch_one = scatter_rows(attended_low, out_full, plain, tp_count) + out_shift
    middle = rows_in + gate_one * branch_one
    normed_two, inverse_two = normalize(middle)
    hidden_two = gather_rows(
        (normed_two * (1.0 + scale_two) + shift_two).astype(jnp.bfloat16), tp_count
    )
    up_local = lax.dynamic_slice_in_dim(up_shift, tp_place * hidden_cols, hidden_cols)
    before = plain(hidden_two, up_full) + up_local
    activated, gelu_pull = jax.vjp(gelu_tanh, before)
    activated_low = activated.astype(jnp.bfloat16)
    grad_before = gelu_pull(outer_cols(grad_branch_two, down_full))[0].astype(jnp.bfloat16)
    grad_hidden_two = scatter_rows(grad_before, up_full, outer_cols, tp_count)
    branch_two = scatter_rows(activated_low, down_full, plain, tp_count) + down_shift
    outcome = (middle + gate_two * branch_two).astype(jnp.bfloat16)
    grad_gate_two = jnp.sum(grad_rows * branch_two, axis=0)
    down_bias_part = jnp.sum(grad_two_own.astype(jnp.float32), axis=0)
    down_grad = reduce_grad(inner_rows(activated_low, grad_branch_two), 1)
    up_bias_part = jnp.sum(grad_before.astype(jnp.float32), axis=0)
    up_grad = reduce_grad(inner_rows(hidden_two, grad_before), 0)
    grad_scale_two = jnp.sum(grad_hidden_two * normed_two, axis=0)
    grad_shift_two = jnp.sum(grad_hidden_two, axis=0)
    grad_middle = grad_rows + norm_back(
        grad_hidden_two * (1.0 + scale_two), normed_two, inverse_two
    )
    grad_gate_one = jnp.sum(grad_middle * branch_one, axis=0)
    grad_one_own = (grad_middle * gate_one).astype(jnp.bfloat16)
    grad_branch_one = gather_rows(grad_one_own, tp_count)
    out_bias_part = jnp.sum(grad_one_own.astype(jnp.float32), axis=0)
    out_grad = reduce_grad(inner_rows(attended_low, grad_branch_one), 1)
    grad_attended = outer_cols(grad_branch_one, out_full).astype(jnp.bfloat16)
    grad_blocks = (
        to_heads(grad_attended, head_count)
        .reshape(head_count, block_count, block, HEAD_DIM)
        .transpose(1, 0, 2, 3)
    )

    def attend_back(carry, inputs):
        grad_keys, grad_values = carry
        query_block, log_block, grad_block = inputs
        scores = (
            jnp.einsum("hqd,hkd->hqk", query_block, keys_all, preferred_element_type=jnp.float32)
            * scaling
        )
        weights = jnp.exp(scores - log_block[..., None])
        grad_weights = jnp.einsum(
            "hqd,hkd->hqk", grad_block, values_all, preferred_element_type=jnp.float32
        )
        centered = jnp.sum(weights * grad_weights, axis=-1, keepdims=True)
        grad_scores = (weights * (grad_weights - centered)).astype(jnp.bfloat16)
        grad_query = (
            jnp.einsum("hqk,hkd->hqd", grad_scores, keys_all, preferred_element_type=jnp.float32)
            * scaling
        )
        grad_keys = (
            grad_keys
            + jnp.einsum(
                "hqk,hqd->hkd", grad_scores, query_block, preferred_element_type=jnp.float32
            )
            * scaling
        )
        grad_values = grad_values + jnp.einsum(
            "hqk,hqd->hkd",
            weights.astype(jnp.bfloat16),
            grad_block,
            preferred_element_type=jnp.float32,
        )
        return ((grad_keys, grad_values), grad_query)

    zero_heads = jnp.zeros((head_count, seq_len, HEAD_DIM), jnp.float32)
    (grad_keys, grad_values), grad_query_blocks = lax.scan(
        attend_back, (zero_heads, zero_heads), (query_blocks, log_totals, grad_blocks)
    )
    grad_queries = grad_query_blocks.transpose(1, 0, 2, 3).reshape(head_count, seq_len, HEAD_DIM)
    grad_projected = jnp.stack(
        [from_heads(grad_queries), from_heads(grad_keys), from_heads(grad_values)], axis=1
    ).astype(jnp.bfloat16)
    grad_projected, down_grad, up_grad, out_grad = lax.optimization_barrier(
        (grad_projected, down_grad, up_grad, out_grad)
    )
    qv_bias_part = jnp.sum(grad_projected[:, 0::2].astype(jnp.float32), axis=0)
    grad_flat = grad_projected.reshape(seq_len, 3 * head_cols)
    grad_hidden_one = scatter_rows(grad_flat, qkv_matrix, outer_cols, tp_count)
    qkv_grad = reduce_grad(inner_rows(hidden_one, grad_flat).reshape(width, 3, head_cols), 0)
    grad_scale_one = jnp.sum(grad_hidden_one * normed_one, axis=0)
    grad_shift_one = jnp.sum(grad_hidden_one, axis=0)
    grad_tokens = grad_middle + norm_back(
        grad_hidden_one * (1.0 + scale_one), normed_one, inverse_one
    )
    grad_mod_part = jnp.concatenate(
        [
            grad_shift_one,
            grad_scale_one,
            grad_gate_one,
            grad_shift_two,
            grad_scale_two,
            grad_gate_two,
        ]
    )
    qv_padded = lax.dynamic_update_slice_in_dim(
        jnp.zeros((2, width), jnp.float32), qv_bias_part, tp_place * head_cols, 1
    )
    up_padded = lax.dynamic_update_slice_in_dim(
        jnp.zeros((hidden_full,), jnp.float32), up_bias_part, tp_place * hidden_cols, 0
    )
    packed = jnp.concatenate(
        [
            grad_mod_part.reshape(fsdp_count, mod_thin),
            qv_padded.reshape(2, fsdp_count, thin).transpose(1, 0, 2).reshape(fsdp_count, 2 * thin),
            out_bias_part.reshape(fsdp_count, thin),
            up_padded.reshape(fsdp_count, hidden_thin),
            down_bias_part.reshape(fsdp_count, thin),
        ],
        axis=1,
    )
    traded = sum_pair(trade(packed), tp_count)
    totals = jnp.sum(traded, axis=0)
    grad_mod = traded[:, :mod_thin]
    mod_weight_grad = lax.dot_general(
        silu_low.astype(jnp.float32), grad_mod, (((0,), (0,)), ((), ())), precision=HIGH
    )
    silu_parts = lax.dot_general(
        grad_mod, mod_weight.astype(jnp.float32), (((1,), (1,)), ((), ())), precision=HIGH
    )
    grad_silu = jnp.sum(trade(silu_parts), axis=0)
    cond_row = condition[0].astype(jnp.float32)
    own_part = lax.dynamic_slice_in_dim(cond_row, tp_place * share, share)
    cond_grad = jax.vjp(jax.nn.silu, own_part)[1](grad_silu)[0][None, :]
    spot = mod_thin
    qv_bias_grad = totals[spot : spot + 2 * thin].reshape(2, thin)
    spot += 2 * thin
    out_bias_grad = totals[spot : spot + thin]
    spot += thin
    up_bias_grad = totals[spot : spot + hidden_thin]
    spot += hidden_thin
    down_bias_grad = totals[spot : spot + thin]
    return (
        outcome[None],
        grad_tokens.astype(jnp.bfloat16)[None],
        cond_grad,
        mod_weight_grad,
        totals[:mod_thin],
        qkv_grad.astype(jnp.float32),
        qv_bias_grad,
        out_grad.astype(jnp.float32),
        out_bias_grad,
        up_grad.astype(jnp.float32),
        up_bias_grad,
        down_grad.astype(jnp.float32),
        down_bias_grad,
    )


def solution(mesh):
    return jax.shard_map(
        shards,
        mesh=mesh,
        in_specs=(
            P("fsdp", "tp", None),
            P("fsdp", None),
            P("tp", "fsdp"),
            P("fsdp"),
            P("fsdp", None, "tp"),
            P(None, "fsdp"),
            P("tp", "fsdp"),
            P("fsdp"),
            P("fsdp", "tp"),
            P("fsdp"),
            P("tp", "fsdp"),
            P("fsdp"),
            P("fsdp", "tp", None),
        ),
        out_specs=(
            P("fsdp", "tp", None),
            P("fsdp", "tp", None),
            P("fsdp", "tp"),
            P("tp", "fsdp"),
            P("fsdp"),
            P("fsdp", None, "tp"),
            P(None, "fsdp"),
            P("tp", "fsdp"),
            P("fsdp"),
            P("fsdp", "tp"),
            P("fsdp"),
            P("tp", "fsdp"),
            P("fsdp"),
        ),
        check_vma=False,
    )
```

profile of v0, /device:TPU:0, one launch (start us, length us, event | category | flops | bytes accessed | tf_op | source)
XLA Modules:
  0.0 673.1 jit_solution(11910449368759546914)
XLA Ops:
  13.0 23.3 %all_gather.15 = bf16[128,256]{1,0:T(8,128)(2,1)S(1)} all-gather(bf16[8,256]{1,0:T(8,128)(2,1)S(1)} %reshape.202), channel_id=1, replica_groups=mesh['fsdp'=16,'tp'=2] {'fsdp'}, dimensions={0}, use_global_device_ids=true | all-gather | bytes 69632 | tf_op jit(solution)/shard_map/all_gather | solution.py:87
  44.9 7.1 %all-to-all-done = f32[16,1,432]{2,1,0:T(1,128)S(1)} async-done(((f32[16,1,432]{2,1,0:T(1,128)}), f32[16,1,432]{2,1,0:T(1,128)S(1)}, u32[]{:S(2)}, u32[]{:S(2)}) %all-to-all-start) | async-done | bytes 27680 | tf_op jit(solution)/shard_map/all_to_all | solution.py:91
  55.5 9.6 %all-gather.5.cloned.1.call-done = bf16[1152,3,576]{2,0,1:T(8,128)(2,1)} async-done(((bf16[72,3,576]{2,0,1:T(8,128)(2,1)}), bf16[1152,3,576]{2,0,1:T(8,128)(2,1)}) %all-gather.5.cloned.1.call-update) | async-done | bytes 3981328 | tf_op jit(solution)/shard_map/all_gather | solution.py:123
  65.2 6.8 %copy.44 = bf16[1152,3,576]{0,2,1:T(8,128)(2,1)} copy(bf16[1152,3,576]{2,0,1:T(8,128)(2,1)} %all-gather.5.cloned.1.call-done) | data formatting | bytes 7962624 | tf_op jit(solution)/shard_map/all_gather | solution.py:123
  72.0 8.8 %collective-permute-done.1 = bf16[512,1152]{1,0:T(8,128)(2,1)S(1)} collective-permute-done((bf16[512,1152]{1,0:T(8,128)(2,1)S(1)}, bf16[512,1152]{1,0:T(8,128)(2,1)S(1)}, u32[]{:S(2)}, u32[]{:S(2)}) %collective-permute-start.1) | collective-permute-done | bytes 1179680 | tf_op jit(solution)/shard_map/ppermute | solution.py:50
  81.8 6.6 fusion.40
  96.9 23.9 %while.27 = (s32[]{:T(128)}, bf16[2,8,512,72]{2,3,1,0:T(8,128)(2,1)}, f32[2,8,512]{2,1,0:T(8,128)S(1)}, bf16[2,8,512,72]{2,3,1,0:T(8,128)(2,1)S(1)}, bf16[8,1024...) while((s32[]{:T(128)}, bf16[2,8,512,72]{2,3,1,0:T(8,128)(2,1)}, ...), condition=%wide.region_5.6_spmd, body=%wide.region_2.5_spmd.sunk | while | flops 1245704192 | bytes 68747440 | solution.py:186
  103.2 4.7 fusion.152
  115.1 4.7 fusion.152
  124.2 3.8 convolution_convert_fusion.6
  131.7 23.0 %collective-permute-done.2 = bf16[512,1152]{1,0:T(8,128)(2,1)} collective-permute-done((bf16[512,1152]{1,0:T(8,128)(2,1)}, bf16[512,1152]{1,0:T(8,128)(2,1)}, u32[]{:S(2)}, u32[]{:S(2)}) %collective-permute-start.2) | collective-permute-done | bytes 1179680 | tf_op jit(solution)/shard_map/ppermute | solution.py:50
  154.7 4.9 fusion.103
  168.1 22.9 %collective-permute-done.3 = bf16[512,1152]{1,0:T(8,128)(2,1)} collective-permute-done((bf16[512,1152]{1,0:T(8,128)(2,1)}, bf16[512,1152]{1,0:T(8,128)(2,1)}, u32[]{:S(2)}, u32[]{:S(2)}) %collective-permute-start.3) | collective-permute-done | bytes 1179680 | tf_op jit(solution)/shard_map/ppermute | solution.py:50
  191.0 14.7 %multiply_convert_fusion.1 = (bf16[1024,2304]{1,0:T(8,128)(2,1)}, f32[1024,2304]{1,0:T(8,128)}) fusion(f32[2304]{0:T(1024)S(1)} %dynamic_slice.28, bf16[1152,2304]{1,0:T(8,128)(2,1)} %all-gather.9.cloned.1.call-done, bf16[512,1152]{1,0:T(8,128)(2,1)} %collective-permute-done.3, bf16[512,1152]{1,0:T(8,128)(2,1)} %add_convert_fusion.1), kind=kOutput, calls=%fused_computation.53 | convolution fusion | flops 5464129536 | bytes 21832704 | tf_op jit(solution)/shard_map/dot_general | solution.py:76
  205.7 7.1 %collective-permute-done.5 = bf16[512,1152]{1,0:T(8,128)(2,1)} collective-permute-done((bf16[512,1152]{1,0:T(8,128)(2,1)}, bf16[512,1152]{1,0:T(8,128)(2,1)}, u32[]{:S(2)}, u32[]{:S(2)}) %collective-permute-start.5) | collective-permute-done | bytes 1179680 | tf_op jit(solution)/shard_map/ppermute | solution.py:50
  212.8 6.8 %all-gather.11.cloned.1.call-done = bf16[2304,1152]{0,1:T(8,128)(2,1)} async-done(((bf16[2304,72]{0,1:T(8,128)(2,1)}), bf16[2304,1152]{0,1:T(8,128)(2,1)}) %all-gather.11.cloned.1.call-update) | async-done | bytes 5308432 | tf_op jit(solution)/shard_map/all_gather | solution.py:126
  219.6 17.0 %convert_reduce_fusion = (f32[2304]{0:T(1024)}, bf16[1024,2304]{1,0:T(8,128)(2,1)}) fusion(f32[1024,2304]{1,0:T(8,128)} %get-tuple-element.259, f32[2304]{0:T(1024)S(1)} %dynamic_slice.28, bf16[2304,1152]{0,1:T(8,128)(2,1)} %all-gather.11.cloned.1.call-done, bf16[512,1152]{1,0:T(8,128)(2,1)} %collective-permute-done.5, bf16[512,1152]{1,0:T(8,128)(2,1)} %get-tuple-element.232), kind=kOutput, calls=%fused_computation.52 | convolution fusion | flops 5494798336 | bytes 21841920 | tf_op jit(solution)/shard_map/dot_general | solution.py:32
  236.6 5.0 convolution_convert_fusion.4
  247.1 5.0 fusion.67
  252.1 18.5 %collective-permute-done.6 = bf16[512,1152]{1,0:T(8,128)(2,1)S(1)} collective-permute-done((bf16[512,1152]{1,0:T(8,128)(2,1)S(1)}, bf16[512,1152]{1,0:T(8,128)(2,1)S(1)}, u32[]{:S(2)}, u32[]{:S(2)}) %collective-permute-start.6) | collective-permute-done | bytes 1179680 | tf_op jit(solution)/shard_map/ppermute | solution.py:50
  270.6 6.0 multiply_reduce_fusion.2
  276.5 18.6 %collective-permute-done.4 = bf16[512,1152]{1,0:T(8,128)(2,1)S(1)} collective-permute-done((bf16[512,1152]{1,0:T(8,128)(2,1)S(1)}, bf16[512,1152]{1,0:T(8,128)(2,1)S(1)}, u32[]{:S(2)}, u32[]{:S(2)}) %collective-permute-start.4) | collective-permute-done | bytes 1179680 | tf_op jit(solution)/shard_map/ppermute | solution.py:50
  295.2 4.1 fusion.62
  300.7 25.8 %collective-permute-done.7 = bf16[512,1152]{1,0:T(8,128)(2,1)S(1)} collective-permute-done((bf16[512,1152]{1,0:T(8,128)(2,1)S(1)}, bf16[512,1152]{1,0:T(8,128)(2,1)S(1)}, u32[]{:S(2)}, u32[]{:S(2)}) %collective-permute-start.7) | collective-permute-done | bytes 1179680 | tf_op jit(solution)/shard_map/ppermute | solution.py:50
  331.0 10.7 %convolution_convert_fusion.1 = bf16[2304,1152]{0,1:T(8,128)(2,1)} fusion(bf16[1024,2304]{1,0:T(8,128)(2,1)} %get-tuple-element.258, bf16[512,1152]{1,0:T(8,128)(2,1)} %collective-permute-done.5, bf16[512,1152]{1,0:T(8,128)(2,1)} %get-tuple-element.232), kind=kOutput, calls=%fused_computation.44 | convolution fusion | flops 5443190784 | bytes 12386304 | tf_op jit(solution)/shard_map/dot_general | solution.py:26
  341.8 10.7 %convolution_convert_fusion = bf16[1152,2304]{1,0:T(8,128)(2,1)} fusion(bf16[1024,2304]{1,0:T(8,128)(2,1)} %get-tuple-element.263, bf16[512,1152]{1,0:T(8,128)(2,1)} %collective-permute-done.3, bf16[512,1152]{1,0:T(8,128)(2,1)} %add_convert_fusion.1), kind=kOutput, calls=%fused_computation.43 | convolution fusion | flops 5443190784 | bytes 12386304 | tf_op jit(solution)/shard_map/dot_general | solution.py:26
  352.6 4.8 convolution_convert_fusion.7
  357.4 4.0 reshape.210
  365.0 116.9 %while.28 = (s32[]{:T(128)}, f32[8,1024,72]{1,2,0:T(8,128)}, f32[8,1024,72]{1,2,0:T(8,128)}, bf16[2,8,512,72]{2,3,1,0:T(8,128)(2,1)}, bf16[2,8,512,72]{2,3,1,0:T...) while((s32[]{:T(128)}, f32[8,1024,72]{1,2,0:T(8,128)}, ...), condition=%wide.region_12.13_spmd.clone, body=%wide.region_10.12_spmd.clone.sunk | while | flops 3073470464 | bytes 261996880 | solution.py:258
  365.4 8.1 %fusion.162 = f32[8,512,1024]{2,1,0:T(8,128)} fusion(bf16[8,1024,72]{1,2,0:T(8,128)(2,1)S(1)} %get-tuple-element.414, bf16[2,8,512,72]{2,3,1,0:T(8,128)(2,1)S(1)} %get-tuple-element.413, s32[]{:T(128)S(6)} %copy.83), kind=kOutput, calls=%fused_computation.29.clone.1 | convolution fusion | flops 603979776 | bytes 18546692 | tf_op jit(solution)/shard_map/while/body/eval_jaxpr/hqd,hkd->hqk/dot_general | solution.py:229
  373.5 10.4 %select_add_fusion.5 = f32[8,1024,72]{1,2,0:T(8,128)} fusion(f32[8,1024,72]{1,2,0:T(8,128)} %get-tuple-element.400, f32[8,512,1024]{2,1,0:T(8,128)} %fusion.162, f32[8,512]{1,0:T(8,128)S(1)} %dynamic-slice_bitcast_fusion.2, pred[]{:T(512)S(6)} %compare.4, bf16[2,8,512,72]{2,3,1,0:T(8,128)(2,1)} %get-tuple-element.416, s32[]{:T(128)S(6)} %copy.83), kind=kOutput, calls=%fused_computation.20.clone.1 | convolution fusion | flops 617742336 | bytes 22102020 | tf_op jit(solution)/shard_map/while/body/eval_jaxpr/hqk,hqd->hkd/dot_general | solution.py:249
  383.9 14.6 %multiply_reduce_fusion.11 = (f32[8,512]{1,0:T(8,128)S(1)}, f32[8,512,1024]{2,1,0:T(8,128)}) fusion(f32[8,512,1024]{2,1,0:T(8,128)} %fusion.162, f32[8,512]{1,0:T(8,128)S(1)} %dynamic-slice_bitcast_fusion.2, bf16[8,1024,72]{1,2,0:T(8,128)(2,1)} %get-tuple-element.417, bf16[2,8,512,72]{2,3,1,0:T(8,128)(2,1)} %get-tuple-element.416, s32[]{:T(128)S(6)} %copy.83), kind=kOutput, calls=%fused_computation.14.clone.1 | convolution fusion | flops 620752896 | bytes 35356676 | tf_op jit(solution)/shard_map/while/body/eval_jaxpr/hqd,hkd->hqk/dot_general | solution.py:233
  401.2 11.2 %multiply_convert_fusion.8 = bf16[8,512,1024]{2,1,0:T(8,128)(2,1)} fusion(f32[8,512,1024]{2,1,0:T(8,128)} %get-tuple-element.364, f32[8,512,1024]{2,1,0:T(8,128)S(1)} %copy-done.1, f32[8,512]{1,0:T(8,128)S(1)} %get-tuple-element.365, f32[8,512]{1,0:T(8,128)S(1)} %dynamic-slice_bitcast_fusion.2), kind=kLoop, calls=%fused_computation.13.clone.1 | loop fusion | flops 20971520 | bytes 41975808 | tf_op jit(solution)/shard_map/while/body/eval_jaxpr/convert_element_type | solution.py:237
  412.5 7.3 %fusion.163 = bf16[2,8,512,72]{2,3,1,0:T(8,128)(2,1)} fusion(bf16[2,8,512,72]{2,3,1,0:T(8,128)(2,1)} %get-tuple-element.401, s32[]{:T(128)S(6)} %copy.83, bf16[8,512,1024]{2,1,0:T(8,128)(2,1)} %multiply_convert_fusion.8, bf16[8,1024,72]{1,2,0:T(8,128)(2,1)} %copy-done.3), kind=kOutput, calls=%fused_computation.24.clone.1 | convolution fusion | flops 604274688 | bytes 10747908 | tf_op jit(solution)/shard_map/while/body/eval_jaxpr/hqk,hkd->hqd/dot_general | solution.py:239
  422.9 8.1 %fusion.162 = f32[8,512,1024]{2,1,0:T(8,128)} fusion(bf16[8,1024,72]{1,2,0:T(8,128)(2,1)S(1)} %get-tuple-element.414, bf16[2,8,512,72]{2,3,1,0:T(8,128)(2,1)S(1)} %get-tuple-element.413, s32[]{:T(128)S(6)} %copy.83), kind=kOutput, calls=%fused_computation.29.clone.1 | convolution fusion | flops 603979776 | bytes 18546692 | tf_op jit(solution)/shard_map/while/body/eval_jaxpr/hqd,hkd->hqk/dot_general | solution.py:229
  431.1 11.1 %select_add_fusion.5 = f32[8,1024,72]{1,2,0:T(8,128)} fusion(f32[8,1024,72]{1,2,0:T(8,128)} %get-tuple-element.400, f32[8,512,1024]{2,1,0:T(8,128)} %fusion.162, f32[8,512]{1,0:T(8,128)S(1)} %dynamic-slice_bitcast_fusion.2, pred[]{:T(512)S(6)} %compare.4, bf16[2,8,512,72]{2,3,1,0:T(8,128)(2,1)} %get-tuple-element.416, s32[]{:T(128)S(6)} %copy.83), kind=kOutput, calls=%fused_computation.20.clone.1 | convolution fusion | flops 617742336 | bytes 22102020 | tf_op jit(solution)/shard_map/while/body/eval_jaxpr/hqk,hqd->hkd/dot_general | solution.py:249
  442.2 14.6 %multiply_reduce_fusion.11 = (f32[8,512]{1,0:T(8,128)S(1)}, f32[8,512,1024]{2,1,0:T(8,128)}) fusion(f32[8,512,1024]{2,1,0:T(8,128)} %fusion.162, f32[8,512]{1,0:T(8,128)S(1)} %dynamic-slice_bitcast_fusion.2, bf16[8,1024,72]{1,2,0:T(8,128)(2,1)} %get-tuple-element.417, bf16[2,8,512,72]{2,3,1,0:T(8,128)(2,1)} %get-tuple-element.416, s32[]{:T(128)S(6)} %copy.83), kind=kOutput, calls=%fused_computation.14.clone.1 | convolution fusion | flops 620752896 | bytes 35356676 | tf_op jit(solution)/shard_map/while/body/eval_jaxpr/hqd,hkd->hqk/dot_general | solution.py:233
  459.2 10.5 %multiply_convert_fusion.8 = bf16[8,512,1024]{2,1,0:T(8,128)(2,1)} fusion(f32[8,512,1024]{2,1,0:T(8,128)} %get-tuple-element.364, f32[8,512,1024]{2,1,0:T(8,128)S(1)} %copy-done.1, f32[8,512]{1,0:T(8,128)S(1)} %get-tuple-element.365, f32[8,512]{1,0:T(8,128)S(1)} %dynamic-slice_bitcast_fusion.2), kind=kLoop, calls=%fused_computation.13.clone.1 | loop fusion | flops 20971520 | bytes 41975808 | tf_op jit(solution)/shard_map/while/body/eval_jaxpr/convert_element_type | solution.py:237
  469.7 7.3 %fusion.163 = bf16[2,8,512,72]{2,3,1,0:T(8,128)(2,1)} fusion(bf16[2,8,512,72]{2,3,1,0:T(8,128)(2,1)} %get-tuple-element.401, s32[]{:T(128)S(6)} %copy.83, bf16[8,512,1024]{2,1,0:T(8,128)(2,1)} %multiply_convert_fusion.8, bf16[8,1024,72]{1,2,0:T(8,128)(2,1)} %copy-done.3), kind=kOutput, calls=%fused_computation.24.clone.1 | convolution fusion | flops 604274688 | bytes 10747908 | tf_op jit(solution)/shard_map/while/body/eval_jaxpr/hqk,hkd->hqd/dot_general | solution.py:239
  477.0 4.9 select_add_fusion.4
  488.0 65.6 %reduce-scatter.11.cloned.1.call-done = bf16[72,2304]{1,0:T(8,128)(2,1)} async-done(((bf16[1152,2304]{1,0:T(8,128)(2,1)}), bf16[72,2304]{1,0:T(8,128)(2,1)}) %reduce-scatter.11.cloned.1.call-update) | async-done | bytes 331792 | tf_op jit(solution)/shard_map/reduce_scatter | solution.py:80
  553.6 7.6 %convolution_convert_fusion.2 = bf16[1152,3,576]{2,0,1:T(8,128)(2,1)S(1)} fusion(bf16[1024,3,576]{0,2,1:T(8,128)(2,1)} %pad_maximum_fusion, bf16[512,1152]{1,0:T(8,128)(2,1)S(1)} %copy-done.56, bf16[512,1152]{1,0:T(8,128)(2,1)S(1)} %copy-done.24), kind=kOutput, calls=%fused_computation.54 | convolution fusion | flops 4083572736 | bytes 9879552 | tf_op jit(solution)/shard_map/dot_general | solution.py:26
  561.3 18.2 %copy.56 = bf16[1152,3,576]{2,1,0:T(4,128)(2,1)} copy(bf16[1152,3,576]{2,0,1:T(8,128)(2,1)S(1)} %convolution_convert_fusion.2) | data formatting | bytes 7962624
  579.5 12.3 %reshape.225 = bf16[1152,1728]{1,0:T(8,128)(2,1)} reshape(bf16[1152,3,576]{2,1,0:T(4,128)(2,1)} %copy.56) | data formatting | bytes 7962624
  591.8 6.8 %fusion.43 = bf16[512,1152]{1,0:T(8,128)(2,1)} fusion(bf16[1152,3,576]{2,0,1:T(8,128)(2,1)} %all-gather.5.cloned.1.call-done, bf16[1024,3,576]{0,2,1:T(8,128)(2,1)} %pad_maximum_fusion), kind=kOutput, calls=%fused_computation.66 | convolution fusion | flops 2039021568 | bytes 7372800 | tf_op jit(solution)/shard_map/dot_general | solution.py:32
  603.7 21.7 %collective-permute-done.8 = bf16[512,1152]{1,0:T(8,128)(2,1)} collective-permute-done((bf16[512,1152]{1,0:T(8,128)(2,1)}, bf16[512,1152]{1,0:T(8,128)(2,1)}, u32[]{:S(2)}, u32[]{:S(2)}) %collective-permute-start.8) | collective-permute-done | bytes 1179680 | tf_op jit(solution)/shard_map/ppermute | solution.py:50
  625.4 6.9 %fusion.59 = (f32[1152]{0:T(1024)S(1)}, f32[512]{0:T(512)S(1)}, f32[512]{0:T(512)S(1)}, f32[1152]{0:T(1024)S(1)}, f32[512,1152]{1,0:T(8,128)S(1)}) fusion(bf16[1,512,1152]{2,1,0:T(8,128)(2,1)S(1)} %copy-done.13, f32[512]{0:T(512)S(1)} %copy-done.48, f32[512]{0:T(512)S(1)} %copy-done.44, f32[1152]{0:T(1024)S(1)} %copy-done.35, ...), kind=kOutput, calls=%fused_computation.87 | convolution fusion | flops 2045506304 | bytes 10933760 | tf_op jit(solution)/shard_map/dot_general | solution.py:32
  636.3 11.1 %all_to_all.30 = f32[16,1,1008]{2,1,0:T(1,128)S(1)} all-to-all(f32[16,1,1008]{2,1,0:T(1,128)S(1)} %all_to_all.22), channel_id=1, replica_groups=mesh['fsdp'=16,'tp'=2] {'fsdp'}, dimensions={0} | all-to-all | bytes 129024 | tf_op jit(solution)/shard_map/all_to_all | solution.py:91
  (282 shorter events, 113.9 us)
Async XLA Ops:
  7.2 29.3 %copy-start = (bf16[576,432]{0,1:T(8,128)(2,1)S(1)}, bf16[576,432]{0,1:T(8,128)(2,1)}, u32[]{:S(2)}) copy-start(bf16[576,432]{0,1:T(8,128)(2,1)} %param.19) | copy-start | bytes 1492996
  7.2 31.1 %copy-start.12 = (bf16[1,512,1152]{2,1,0:T(8,128)(2,1)S(1)}, bf16[1,512,1152]{2,1,0:T(8,128)(2,1)}, u32[]{:S(2)}) copy-start(bf16[1,512,1152]{2,1,0:T(8,128)(2,1)} %param.17) | copy-start | bytes 3538948
  7.2 31.8 %copy-start.52 = (bf16[432]{0:T(512)(128)(2,1)S(1)}, bf16[432]{0:T(512)(128)(2,1)}, u32[]{:S(2)}) copy-start(bf16[432]{0:T(512)(128)(2,1)} %param.20) | copy-start | bytes 2596
  7.2 57.9 %all-gather.5.cloned.1.call-start = ((), (), s32[]{:S(2)}) async-start(), calls=%async_computation.7 | async-start | bytes 4700160 | tf_op jit(solution)/shard_map/all_gather | solution.py:123
  8.0 116.3 %all-gather.7.cloned.1.call-start = ((), (), s32[]{:S(2)}) async-start(), calls=%async_computation.8 | async-start | bytes 1566720 | tf_op jit(solution)/shard_map/all_gather | solution.py:124
  8.7 182.3 %all-gather.9.cloned.1.call-start = ((), (), s32[]{:S(2)}) async-start(), calls=%async_computation.9 | async-start | bytes 5640192 | tf_op jit(solution)/shard_map/all_gather | solution.py:125
  36.4 18.6 %copy-start.25 = (f32[16,1728]{1,0:T(8,128)}, f32[16,1728]{1,0:T(8,128)S(1)}, u32[]{:S(2)}) copy-start(f32[16,1728]{1,0:T(8,128)S(1)} %slice_convert_fusion.1) | copy-start | bytes 331780
  36.8 3.9 collective-permute-start
  41.4 10.7 %all-to-all-start = ((f32[16,1,432]{2,1,0:T(1,128)}), f32[16,1,432]{2,1,0:T(1,128)S(1)}, u32[]{:S(2)}, u32[]{:S(2)}) async-start(f32[16,1,432]{2,1,0:T(1,128)} %copy.43), calls=%async_computation | async-start | bytes 65536 | tf_op jit(solution)/shard_map/all_to_all | solution.py:91
  44.9 174.8 %all-gather.11.cloned.1.call-start = ((), (), s32[]{:S(2)}) async-start(), calls=%async_computation.10 | async-start | bytes 5640192 | tf_op jit(solution)/shard_map/all_gather | solution.py:126
  53.5 27.3 %copy-start.23 = (bf16[512,1152]{1,0:T(8,128)(2,1)}, bf16[512,1152]{1,0:T(8,128)(2,1)S(1)}, u32[]{:S(2)}) copy-start(bf16[512,1152]{1,0:T(8,128)(2,1)S(1)} %fusion.53) | copy-start | bytes 3538948
  53.5 27.3 %collective-permute-start.1 = (bf16[512,1152]{1,0:T(8,128)(2,1)S(1)}, bf16[512,1152]{1,0:T(8,128)(2,1)S(1)}, u32[]{:S(2)}, u32[]{:S(2)}) collective-permute-start(bf16[512,1152]{1,0:T(8,128)(2,1)S(1)} %fusion.53), channel_id=1, source_target_pairs={{0,1},{1,0},{2,3},{3,2},{4,5},{5,4},{6,7},{7,6},{8,9},{9,8},{10,11... | collective-permute-start | bytes 3538952 | tf_op jit(solution)/shard_map/ppermute | solution.py:50
  55.0 433.0 %reduce-scatter.15.cloned.1.call-start = ((), (), s32[]{:S(2)}) async-start(), calls=%async_computation.14 | async-start | bytes 1566720
  124.2 30.5 %copy-start.33 = (f32[1152]{0:T(1024)S(1)}, f32[1152]{0:T(1024)}, u32[]{:S(2)}) copy-start(f32[1152]{0:T(1024)} %get-tuple-element.196) | copy-start | bytes 13828
  128.0 26.7 %collective-permute-start.2 = (bf16[512,1152]{1,0:T(8,128)(2,1)}, bf16[512,1152]{1,0:T(8,128)(2,1)}, u32[]{:S(2)}, u32[]{:S(2)}) collective-permute-start(bf16[512,1152]{1,0:T(8,128)(2,1)} %convolution_convert_fusion.6), channel_id=1, source_target_pairs={{0,1},{1,0},{2,3},{3,2},{4,5},{5,4},{6,7},{7,6},{8,9},{9,8},{10,11... | collective-permute-start | bytes 3538952 | tf_op jit(solution)/shard_map/ppermute | solution.py:50
  131.7 27.9 %copy-start.36 = (f32[1152]{0:T(1024)}, f32[1152]{0:T(1024)S(1)}, u32[]{:S(2)}) copy-start(f32[1152]{0:T(1024)S(1)} %add.213) | copy-start | bytes 13828
  161.8 29.2 %collective-permute-start.3 = (bf16[512,1152]{1,0:T(8,128)(2,1)}, bf16[512,1152]{1,0:T(8,128)(2,1)}, u32[]{:S(2)}, u32[]{:S(2)}) collective-permute-start(bf16[512,1152]{1,0:T(8,128)(2,1)} %add_convert_fusion.1), channel_id=1, source_target_pairs={{0,1},{1,0},{2,3},{3,2},{4,5},{5,4},{6,7},{7,6},{8,9},{9,8},{10,11... | collective-permute-start | bytes 3538952 | tf_op jit(solution)/shard_map/ppermute | solution.py:50
  167.5 45.3 %collective-permute-start.5 = (bf16[512,1152]{1,0:T(8,128)(2,1)}, bf16[512,1152]{1,0:T(8,128)(2,1)}, u32[]{:S(2)}, u32[]{:S(2)}) collective-permute-start(bf16[512,1152]{1,0:T(8,128)(2,1)} %get-tuple-element.232), channel_id=1, source_target_pairs={{0,1},{1,0},{2,3},{3,2},{4,5},{5,4},{6,7},{7,6},{8,9},{9,8},{10,11... | collective-permute-start | bytes 3538952 | tf_op jit(solution)/shard_map/ppermute | solution.py:50
  219.6 17.0 %copy-start.53 = (bf16[1152,2304]{1,0:T(8,128)(2,1)S(1)}, bf16[1152,2304]{1,0:T(8,128)(2,1)}, u32[]{:S(2)}) copy-start(bf16[1152,2304]{1,0:T(8,128)(2,1)} %all-gather.9.cloned.1.call-done) | copy-start | bytes 15925252
  241.7 28.9 %collective-permute-start.6 = (bf16[512,1152]{1,0:T(8,128)(2,1)S(1)}, bf16[512,1152]{1,0:T(8,128)(2,1)S(1)}, u32[]{:S(2)}, u32[]{:S(2)}) collective-permute-start(bf16[512,1152]{1,0:T(8,128)(2,1)S(1)} %convolution_convert_fusion.4), channel_id=1, source_target_pairs={{0,1},{1,0},{2,3},{3,2},{4,5},{5,4},{6,7},{7,6},{8,9},{9,8},{10,11... | collective-permute-start | bytes 3538952 | tf_op jit(solution)/shard_map/ppermute | solution.py:50
  246.5 24.1 %copy-start.11 = (f32[512,1152]{1,0:T(8,128)S(1)}, f32[512,1152]{1,0:T(8,128)}, u32[]{:S(2)}) copy-start(f32[512,1152]{1,0:T(8,128)} %copy-done.10) | copy-start | bytes 7077892
  246.5 48.7 %collective-permute-start.4 = (bf16[512,1152]{1,0:T(8,128)(2,1)S(1)}, bf16[512,1152]{1,0:T(8,128)(2,1)S(1)}, u32[]{:S(2)}, u32[]{:S(2)}) collective-permute-start(bf16[512,1152]{1,0:T(8,128)(2,1)S(1)} %convolution_convert_fusion.5), channel_id=1, source_target_pairs={{0,1},{1,0},{2,3},{3,2},{4,5},{5,4},{6,7},{7,6},{8,9},{9,8},{10,11... | collective-permute-start | bytes 3538952 | tf_op jit(solution)/shard_map/ppermute | solution.py:50
  252.1 43.1 %copy-start.17 = (bf16[1,512,1152]{2,1,0:T(8,128)(2,1)S(1)}, bf16[1,512,1152]{2,1,0:T(8,128)(2,1)}, u32[]{:S(2)}) copy-start(bf16[1,512,1152]{2,1,0:T(8,128)(2,1)} %param.29) | copy-start | bytes 3538948
  295.2 32.5 %copy-start.19 = (bf16[2,8,9,8,512]{4,3,0,2,1:T(8,128)(2,1)S(1)}, bf16[2,8,9,8,512]{4,3,0,2,1:T(8,128)(2,1)}, u32[]{:S(2)}) copy-start(bf16[2,8,9,8,512]{4,3,0,2,1:T(8,128)(2,1)} %copy-done.18) | copy-start | bytes 3538948
  299.2 27.3 %copy-start.22 = (bf16[512,1152]{1,0:T(8,128)(2,1)}, bf16[512,1152]{1,0:T(8,128)(2,1)S(1)}, u32[]{:S(2)}) copy-start(bf16[512,1152]{1,0:T(8,128)(2,1)S(1)} %get-tuple-element.247) | copy-start | bytes 3538948
  299.2 27.3 %collective-permute-start.7 = (bf16[512,1152]{1,0:T(8,128)(2,1)S(1)}, bf16[512,1152]{1,0:T(8,128)(2,1)S(1)}, u32[]{:S(2)}, u32[]{:S(2)}) collective-permute-start(bf16[512,1152]{1,0:T(8,128)(2,1)S(1)} %get-tuple-element.247), channel_id=1, source_target_pairs={{0,1},{1,0},{2,3},{3,2},{4,5},{5,4},{6,7},{7,6},{8,9},{9,8},{10,11... | collective-permute-start | bytes 3538952 | tf_op jit(solution)/shard_map/ppermute | solution.py:50
  331.0 157.0 %reduce-scatter.9.cloned.1.call-start = ((), (), s32[]{:S(2)}) async-start(), calls=%async_computation.11 | async-start | bytes 5640192 | tf_op jit(solution)/shard_map/reduce_scatter | solution.py:80
  341.7 211.9 %reduce-scatter.11.cloned.1.call-start = ((), (), s32[]{:S(2)}) async-start(), calls=%async_computation.12 | async-start | bytes 5640192 | tf_op jit(solution)/shard_map/reduce_scatter | solution.py:80
  352.5 311.5 %reduce-scatter.13.cloned.1.call-start = ((), (), s32[]{:S(2)}) async-start(), calls=%async_computation.13 | async-start | bytes 4386816
  383.9 17.3 %copy-start.1 = (f32[8,512,1024]{2,1,0:T(8,128)S(1)}, f32[8,512,1024]{2,1,0:T(8,128)}, u32[]{:S(2)}) copy-start(f32[8,512,1024]{2,1,0:T(8,128)} %fusion.162) | copy-start | bytes 50331652 | tf_op jit(solution)/shard_map/while
  442.2 17.0 %copy-start.1 = (f32[8,512,1024]{2,1,0:T(8,128)S(1)}, f32[8,512,1024]{2,1,0:T(8,128)}, u32[]{:S(2)}) copy-start(f32[8,512,1024]{2,1,0:T(8,128)} %fusion.162) | copy-start | bytes 50331652 | tf_op jit(solution)/shard_map/while
  485.7 67.9 %copy-start.24 = (bf16[512,1152]{1,0:T(8,128)(2,1)S(1)}, bf16[512,1152]{1,0:T(8,128)(2,1)}, u32[]{:S(2)}) copy-start(bf16[512,1152]{1,0:T(8,128)(2,1)} %copy-done.23) | copy-start | bytes 3538948
  485.7 67.9 %copy-start.56 = (bf16[512,1152]{1,0:T(8,128)(2,1)S(1)}, bf16[512,1152]{1,0:T(8,128)(2,1)}, u32[]{:S(2)}) copy-start(bf16[512,1152]{1,0:T(8,128)(2,1)} %copy-done.55) | copy-start | bytes 3538948
  598.6 26.7 %copy-start.13 = (bf16[1,512,1152]{2,1,0:T(8,128)(2,1)S(1)}, bf16[1,512,1152]{2,1,0:T(8,128)(2,1)}, u32[]{:S(2)}) copy-start(bf16[1,512,1152]{2,1,0:T(8,128)(2,1)} %param.17) | copy-start | bytes 3538948
  598.6 26.7 %copy-start.35 = (f32[1152]{0:T(1024)S(1)}, f32[1152]{0:T(1024)}, u32[]{:S(2)}) copy-start(f32[1152]{0:T(1024)} %copy-done.34) | copy-start | bytes 13828
  598.6 26.7 %copy-start.44 = (f32[512]{0:T(512)S(1)}, f32[512]{0:T(512)}, u32[]{:S(2)}) copy-start(f32[512]{0:T(512)} %copy-done.43) | copy-start | bytes 6148
  598.6 26.7 %copy-start.48 = (f32[512]{0:T(512)S(1)}, f32[512]{0:T(512)}, u32[]{:S(2)}) copy-start(f32[512]{0:T(512)} %copy-done.47) | copy-start | bytes 6148
  598.6 26.7 %collective-permute-start.8 = (bf16[512,1152]{1,0:T(8,128)(2,1)}, bf16[512,1152]{1,0:T(8,128)(2,1)}, u32[]{:S(2)}, u32[]{:S(2)}) collective-permute-start(bf16[512,1152]{1,0:T(8,128)(2,1)} %fusion.43), channel_id=1, source_target_pairs={{0,1},{1,0},{2,3},{3,2},{4,5},{5,4},{6,7},{7,6},{8,9},{9,8},{10,11... | collective-permute-start | bytes 3538952 | tf_op jit(solution)/shard_map/ppermute | solution.py:50
  603.7 28.7 %copy-start.14 = (f32[512,1152]{1,0:T(8,128)S(1)}, f32[512,1152]{1,0:T(8,128)}, u32[]{:S(2)}) copy-start(f32[512,1152]{1,0:T(8,128)} %get-tuple-element.257) | copy-start | bytes 7077892
  603.7 28.7 %copy-start.16 = (f32[512,1152]{1,0:T(8,128)S(1)}, f32[512,1152]{1,0:T(8,128)}, u32[]{:S(2)}) copy-start(f32[512,1152]{1,0:T(8,128)} %get-tuple-element.248) | copy-start | bytes 7077892
  603.7 28.7 %copy-start.37 = (f32[1152]{0:T(1024)S(1)}, f32[1152]{0:T(1024)}, u32[]{:S(2)}) copy-start(f32[1152]{0:T(1024)} %copy-done.36) | copy-start | bytes 13828
  632.4 16.6 %copy-start.30 = (bf16[576,72]{0,1:T(8,128)(2,1)S(1)}, bf16[576,72]{0,1:T(8,128)(2,1)}, u32[]{:S(2)}) copy-start(bf16[576,72]{0,1:T(8,128)(2,1)} %reduce-scatter.15.cloned.1.call-done) | copy-start | bytes 248836
  632.4 17.2 %copy-start.27 = (bf16[72,2304]{1,0:T(8,128)(2,1)S(1)}, bf16[72,2304]{1,0:T(8,128)(2,1)}, u32[]{:S(2)}) copy-start(bf16[72,2304]{1,0:T(8,128)(2,1)} %reduce-scatter.11.cloned.1.call-done) | copy-start | bytes 995332
  632.4 18.1 %copy-start.26 = (bf16[2304,72]{0,1:T(8,128)(2,1)S(1)}, bf16[2304,72]{0,1:T(8,128)(2,1)}, u32[]{:S(2)}) copy-start(bf16[2304,72]{0,1:T(8,128)(2,1)} %reduce-scatter.9.cloned.1.call-done) | copy-start | bytes 995332
  636.0 20.4 %copy-start.29 = (f32[16,1152]{1,0:T(8,128)S(1)}, f32[16,1152]{1,0:T(8,128)}, u32[]{:S(2)}) copy-start(f32[16,1152]{1,0:T(8,128)} %copy-done.28) | copy-start | bytes 221188
  636.3 27.0 %copy-start.46 = (bf16[1152]{0:T(1024)(128)(2,1)S(1)}, bf16[1152]{0:T(1024)(128)(2,1)}, u32[]{:S(2)}) copy-start(bf16[1152]{0:T(1024)(128)(2,1)} %copy-done.45) | copy-start | bytes 6916
  647.4 4.3 collective-permute-start.9
  652.8 10.4 %all-to-all-start.2 = ((f32[16,1,576]{2,1,0:T(1,128)}), f32[16,1,576]{2,1,0:T(1,128)S(1)}, u32[]{:S(2)}, u32[]{:S(2)}) async-start(f32[16,1,576]{2,1,0:T(1,128)} %copy.52), calls=%async_computation.4 | async-start | bytes 81920 | tf_op jit(solution)/shard_map/all_to_all | solution.py:91
  (40 other events, 204.1 us)
Sparse Core Ops, SparseCore 0:
  10.2 54.8 all-gather.4
  67.3 37.8 all-gather.6
  107.4 55.2 all-gather.8
  164.7 54.9 all-gather.10
  331.1 57.3 reduce-scatter.14
  392.4 78.4 reduce-scatter.8
  474.9 78.6 reduce-scatter.10
  591.9 71.8 reduce-scatter.12
where the time goes:
time: 677 us; the launch traced here: 673 us
  waiting for transfers between devices  243 us (36%)
  matrix products  223 us (33%)
  local copies, waits for them, and re-layouts  82.4 us (12%)
  other arithmetic  54.2 us (8%)
  blocking collectives  34.5 us (5%)
  starting transfers between devices  20.5 us (3%)
  between operations  15.1 us (2%)
    ppermute x10, waiting for transfers between devices, swap(): return lax.ppermute(values, 'tp', [(0, 1), (1, 0)])  149 us
    reduce_scatter x2, waiting for transfers between devices, reduce_grad(): lax.psum_scatter(term.astype(jnp.bfloat16), 'fsdp', scatter_dimension=axi...  65.6 us
    dot_general x6, matrix products, outer_cols(): lax.dot_general(left, right, (((1,), (1,)), ((), ())), preferred_element_...  46.6 us
    unnamed x110, local copies, waits for them, and re-layouts  40.1 us
    dot_general x6, matrix products, plain(): return jnp.dot(left, right, preferred_element_type=jnp.float32)  38.1 us
    dot_general x4, matrix products, inner_rows(): lax.dot_general(left, right, (((0,), (0,)), ((), ())), preferred_element_...  32.3 us
    dot_general x2, matrix products, attend_back(): jnp.einsum('hqd,hkd->hqk', grad_block, values_all, preferred_element_type...  29.2 us
    all_gather x1, blocking collectives, gather_small(): lax.all_gather(block, 'fsdp', axis=0, tiled=True).reshape(-1, padded)  23.3 us
  transfers between devices with their start and end apart: 20, of which 15 were waited for; matrix products, arithmetic and copies ran while one was open for 41% of the time, Pallas kernels for 0%

commit v1 on v0

--- a/solution.py
+++ b/solution.py
@@ -1,12 +1,42 @@
+import functools
 import math
 import jax
 import jax.numpy as jnp
 from jax import lax
 from jax.sharding import PartitionSpec as P
+from jax.lax import axis_index, axis_size, ppermute
 
 HEAD_DIM = 72
 EPSILON = 1e-06
 HIGH = lax.Precision.HIGHEST
+
+
+def choose_lane(own_rows, link_axis):
+    current_arr = axis_size(link_axis)
+    finding = axis_index(link_axis)
+    e_now, z, wide_out = (current_arr, finding, own_rows.shape[0])
+    buffer = []
+    for nth in range(e_now):
+        buffer.append((nth, (nth + 1) % e_now))
+    rack = []
+    for nth in range(e_now):
+        rack.append((nth, (nth - 1) % e_now))
+    inter = jnp.zeros((*own_rows.shape[:0], e_now * wide_out, *own_rows.shape[1:]), own_rows.dtype)
+    inter = lax.dynamic_update_slice_in_dim(inter, own_rows, z * wide_out, axis=0)
+    y_new = res = own_rows
+    x_next = e_now // 2
+    for tick in range(1, x_next + 1):
+        y_new = ppermute(y_new, link_axis, buffer)
+        inter = lax.dynamic_update_slice_in_dim(inter, y_new, (z - tick) % e_now * wide_out, axis=0)
+        if tick < e_now - x_next:
+            res = ppermute(res, axis_name=link_axis, perm=rack)
+            inter = lax.dynamic_update_slice_in_dim(
+                inter, res, (z + tick) % e_now * wide_out, axis=0
+            )
+    return inter
+
+
+meet_indices = functools.partial(choose_lane, link_axis="fsdp")
 
 
 def normalize(values):
@@ -84,7 +114,7 @@
     size = flat.shape[0]
     padded = -(-size // 1024) * 1024
     block = jnp.pad(flat, (0, padded - size)).reshape(8, padded // 8)
-    return lax.all_gather(block, "fsdp", axis=0, tiled=True).reshape(-1, padded)[:, :size]
+    return meet_indices(block).reshape(-1, padded)[:, :size]
 
 
 def trade(rows):

time: 677 us -> 696 us (1.028)
  starting transfers between devices: 20.5 us -> 53 us
  blocking collectives: 34.5 us -> 11.2 us
  waiting for transfers between devices: 243 us -> 250 us
    ppermute x0 -> x15, starting transfers between devices: none -> 32.4 us  [the longest x7 32.4 us: choose_lane(): res = ppermute(res, axis_name=link_axis, perm=rack)]
    all_gather x1 -> x0, blocking collectives: 23.3 us -> none  [gather_small(): lax.all_gather(block, 'fsdp', axis=0, tiled=True).reshape(-1, padded)]
    ppermute x0 -> x15, waiting for transfers between devices: none -> 18 us  [the longest x8 11.5 us: choose_lane(): y_new = ppermute(y_new, link_axis, buffer)]
    all_gather x1, waiting for transfers between devices: 9.64 us -> 0.01 us  [shards(): qkv_full = lax.all_gather(qkv_weight, 'fsdp', axis=0, tiled=True)]
  transfers between devices with their start and end apart: 20 -> 35, of which waited for: 15 -> 20; matrix products, arithmetic and copies ran while one was open for 41% -> 40% of each run, Pallas kernels for 0% -> 0%
where the time goes in v1:
time: 696 us; the launch traced here: 691 us
  waiting for transfers between devices  250 us (36%)
  matrix products  223 us (32%)
  local copies, waits for them, and re-layouts  82.6 us (12%)
  other arithmetic  55.4 us (8%)
  starting transfers between devices  53 us (8%)
  between operations  15.4 us (2%)
  blocking collectives  11.2 us (2%)
    ppermute x10, waiting for transfers between devices, swap(): return lax.ppermute(values, 'tp', [(0, 1), (1, 0)])  153 us
    reduce_scatter x2, waiting for transfers between devices, reduce_grad(): lax.psum_scatter(term.astype(jnp.bfloat16), 'fsdp', scatter_dimension=axi...  67.8 us
    dot_general x6, matrix products, outer_cols(): lax.dot_general(left, right, (((1,), (1,)), ((), ())), preferred_element_...  46.6 us
    unnamed x110, local copies, waits for them, and re-layouts  40 us
    dot_general x6, matrix products, plain(): return jnp.dot(left, right, preferred_element_type=jnp.float32)  37.6 us
    ppermute x7, starting transfers between devices, choose_lane(): res = ppermute(res, axis_name=link_axis, perm=rack)  32.4 us
    dot_general x4, matrix products, inner_rows(): lax.dot_general(left, right, (((0,), (0,)), ((), ())), preferred_element_...  32.4 us
    dot_general x2, matrix products, attend_back(): jnp.einsum('hqd,hkd->hqk', grad_block, values_all, preferred_element_type...  29.1 us
  transfers between devices with their start and end apart: 35, of which 20 were waited for; matrix products, arithmetic and copies ran while one was open for 40% of the time, Pallas kernels for 0%

profile of v1, /device:TPU:0, one launch (start us, length us, event | category | flops | bytes accessed | tf_op | source)
XLA Modules:
  0.0 690.9 jit_solution(7291762531083142735)
XLA Ops:
  13.0 5.5 collective-permute-start.1
  20.2 4.5 collective-permute-start.3
  43.3 4.6 collective-permute-start.11
  49.2 4.5 collective-permute-start.13
  53.8 5.7 collective-permute-done.12
  59.5 5.7 collective-permute-done.14
  73.8 6.7 all-to-all-done
  83.9 7.1 %copy.44 = bf16[1152,3,576]{0,2,1:T(8,128)(2,1)} copy(bf16[1152,3,576]{2,0,1:T(8,128)(2,1)} %all-gather.5.cloned.1.call-done) | data formatting | bytes 7962624 | tf_op jit(solution)/shard_map/all_gather | solution.py:153
  91.0 18.5 %collective-permute-done.16 = bf16[512,1152]{1,0:T(8,128)(2,1)S(1)} collective-permute-done((bf16[512,1152]{1,0:T(8,128)(2,1)S(1)}, bf16[512,1152]{1,0:T(8,128)(2,1)S(1)}, u32[]{:S(2)}, u32[]{:S(2)}) %collective-permute-start.16) | collective-permute-done | bytes 1179680 | tf_op jit(solution)/shard_map/ppermute | solution.py:80
  110.5 6.5 fusion.40
  125.6 23.9 %while.27 = (s32[]{:T(128)}, bf16[2,8,512,72]{2,3,1,0:T(8,128)(2,1)}, f32[2,8,512]{2,1,0:T(8,128)S(1)}, bf16[2,8,512,72]{2,3,1,0:T(8,128)(2,1)S(1)}, bf16[8,1024...) while((s32[]{:T(128)}, bf16[2,8,512,72]{2,3,1,0:T(8,128)(2,1)}, ...), condition=%wide.region_5.6_spmd, body=%wide.region_2.5_spmd.sunk | while | flops 1245704192 | bytes 68747440 | solution.py:216
  131.9 4.7 fusion.153
  143.8 4.7 fusion.153
  160.3 23.4 %collective-permute-done.17 = bf16[512,1152]{1,0:T(8,128)(2,1)} collective-permute-done((bf16[512,1152]{1,0:T(8,128)(2,1)}, bf16[512,1152]{1,0:T(8,128)(2,1)}, u32[]{:S(2)}, u32[]{:S(2)}) %collective-permute-start.17) | collective-permute-done | bytes 1179680 | tf_op jit(solution)/shard_map/ppermute | solution.py:80
  183.8 4.8 fusion.104
  197.1 22.9 %collective-permute-done.18 = bf16[512,1152]{1,0:T(8,128)(2,1)} collective-permute-done((bf16[512,1152]{1,0:T(8,128)(2,1)}, bf16[512,1152]{1,0:T(8,128)(2,1)}, u32[]{:S(2)}, u32[]{:S(2)}) %collective-permute-start.18) | collective-permute-done | bytes 1179680 | tf_op jit(solution)/shard_map/ppermute | solution.py:80
  220.0 14.3 %multiply_convert_fusion.1 = (bf16[1024,2304]{1,0:T(8,128)(2,1)}, f32[1024,2304]{1,0:T(8,128)}) fusion(f32[2304]{0:T(1024)S(1)} %dynamic_slice.28, bf16[1152,2304]{1,0:T(8,128)(2,1)} %all-gather.9.cloned.1.call-done, bf16[512,1152]{1,0:T(8,128)(2,1)} %collective-permute-done.18, bf16[512,1152]{1,0:T(8,128)(2,1)} %add_convert_fusion.1), kind=kOutput, calls=%fused_computation.53 | convolution fusion | flops 5464129536 | bytes 21832704 | tf_op jit(solution)/shard_map/dot_general | solution.py:106
  234.3 7.9 %collective-permute-done.20 = bf16[512,1152]{1,0:T(8,128)(2,1)} collective-permute-done((bf16[512,1152]{1,0:T(8,128)(2,1)}, bf16[512,1152]{1,0:T(8,128)(2,1)}, u32[]{:S(2)}, u32[]{:S(2)}) %collective-permute-start.20) | collective-permute-done | bytes 1179680 | tf_op jit(solution)/shard_map/ppermute | solution.py:80
  242.2 17.1 %convert_reduce_fusion = (f32[2304]{0:T(1024)}, bf16[1024,2304]{1,0:T(8,128)(2,1)}) fusion(f32[1024,2304]{1,0:T(8,128)} %get-tuple-element.259, f32[2304]{0:T(1024)S(1)} %dynamic_slice.28, bf16[2304,1152]{0,1:T(8,128)(2,1)} %all-gather.11.cloned.1.call-done, bf16[512,1152]{1,0:T(8,128)(2,1)} %collective-permute-done.20, ...), kind=kOutput, calls=%fused_computation.52 | convolution fusion | flops 5494798336 | bytes 21841920 | tf_op jit(solution)/shard_map/dot_general | solution.py:62
  259.3 5.0 convolution_convert_fusion.4
  269.8 5.0 fusion.67
  274.7 18.6 %collective-permute-done.21 = bf16[512,1152]{1,0:T(8,128)(2,1)S(1)} collective-permute-done((bf16[512,1152]{1,0:T(8,128)(2,1)S(1)}, bf16[512,1152]{1,0:T(8,128)(2,1)S(1)}, u32[]{:S(2)}, u32[]{:S(2)}) %collective-permute-start.21) | collective-permute-done | bytes 1179680 | tf_op jit(solution)/shard_map/ppermute | solution.py:80
  293.3 6.0 multiply_reduce_fusion.2
  299.3 15.3 %collective-permute-done.19 = bf16[512,1152]{1,0:T(8,128)(2,1)S(1)} collective-permute-done((bf16[512,1152]{1,0:T(8,128)(2,1)S(1)}, bf16[512,1152]{1,0:T(8,128)(2,1)S(1)}, u32[]{:S(2)}, u32[]{:S(2)}) %collective-permute-start.19) | collective-permute-done | bytes 1179680 | tf_op jit(solution)/shard_map/ppermute | solution.py:80
  320.1 22.5 %collective-permute-done.22 = bf16[512,1152]{1,0:T(8,128)(2,1)S(1)} collective-permute-done((bf16[512,1152]{1,0:T(8,128)(2,1)S(1)}, bf16[512,1152]{1,0:T(8,128)(2,1)S(1)}, u32[]{:S(2)}, u32[]{:S(2)}) %collective-permute-start.22) | collective-permute-done | bytes 1179680 | tf_op jit(solution)/shard_map/ppermute | solution.py:80
  347.0 10.9 %convolution_convert_fusion.1 = bf16[2304,1152]{0,1:T(8,128)(2,1)} fusion(bf16[1024,2304]{1,0:T(8,128)(2,1)} %get-tuple-element.258, bf16[512,1152]{1,0:T(8,128)(2,1)} %collective-permute-done.20, bf16[512,1152]{1,0:T(8,128)(2,1)} %get-tuple-element.232), kind=kOutput, calls=%fused_computation.44 | convolution fusion | flops 5443190784 | bytes 12386304 | tf_op jit(solution)/shard_map/dot_general | solution.py:56
  358.0 10.5 %convolution_convert_fusion = bf16[1152,2304]{1,0:T(8,128)(2,1)} fusion(bf16[1024,2304]{1,0:T(8,128)(2,1)} %get-tuple-element.263, bf16[512,1152]{1,0:T(8,128)(2,1)} %collective-permute-done.18, bf16[512,1152]{1,0:T(8,128)(2,1)} %add_convert_fusion.1), kind=kOutput, calls=%fused_computation.43 | convolution fusion | flops 5443190784 | bytes 12386304 | tf_op jit(solution)/shard_map/dot_general | solution.py:56
  368.6 4.8 convolution_convert_fusion.7
  381.0 116.6 %while.28 = (s32[]{:T(128)}, f32[8,1024,72]{1,2,0:T(8,128)}, f32[8,1024,72]{1,2,0:T(8,128)}, bf16[2,8,512,72]{2,3,1,0:T(8,128)(2,1)}, bf16[2,8,512,72]{2,3,1,0:T...) while((s32[]{:T(128)}, f32[8,1024,72]{1,2,0:T(8,128)}, ...), condition=%wide.region_12.13_spmd.clone, body=%wide.region_10.12_spmd.clone.sunk | while | flops 3073470464 | bytes 261996880 | solution.py:288
  381.2 8.1 %fusion.163 = f32[8,512,1024]{2,1,0:T(8,128)} fusion(bf16[8,1024,72]{1,2,0:T(8,128)(2,1)S(1)} %get-tuple-element.414, bf16[2,8,512,72]{2,3,1,0:T(8,128)(2,1)S(1)} %get-tuple-element.413, s32[]{:T(128)S(6)} %copy.99), kind=kOutput, calls=%fused_computation.29.clone.1 | convolution fusion | flops 603979776 | bytes 18546692 | tf_op jit(solution)/shard_map/while/body/eval_jaxpr/hqd,hkd->hqk/dot_general | solution.py:259
  389.4 10.4 %select_add_fusion.5 = f32[8,1024,72]{1,2,0:T(8,128)} fusion(f32[8,1024,72]{1,2,0:T(8,128)} %get-tuple-element.400, f32[8,512,1024]{2,1,0:T(8,128)} %fusion.163, f32[8,512]{1,0:T(8,128)S(1)} %dynamic-slice_bitcast_fusion.2, pred[]{:T(512)S(6)} %compare.19, bf16[2,8,512,72]{2,3,1,0:T(8,128)(2,1)} %get-tuple-element.416, s32[]{:T(128)S(6)} %copy.99), kind=kOutput, calls=%fused_computation.20.clone.1 | convolution fusion | flops 617742336 | bytes 22102020 | tf_op jit(solution)/shard_map/while/body/eval_jaxpr/hqk,hqd->hkd/dot_general | solution.py:279
  399.8 14.6 %multiply_reduce_fusion.11 = (f32[8,512]{1,0:T(8,128)S(1)}, f32[8,512,1024]{2,1,0:T(8,128)}) fusion(f32[8,512,1024]{2,1,0:T(8,128)} %fusion.163, f32[8,512]{1,0:T(8,128)S(1)} %dynamic-slice_bitcast_fusion.2, bf16[8,1024,72]{1,2,0:T(8,128)(2,1)} %get-tuple-element.417, bf16[2,8,512,72]{2,3,1,0:T(8,128)(2,1)} %get-tuple-element.416, s32[]{:T(128)S(6)} %copy.99), kind=kOutput, calls=%fused_computation.14.clone.1 | convolution fusion | flops 620752896 | bytes 35356676 | tf_op jit(solution)/shard_map/while/body/eval_jaxpr/hqd,hkd->hqk/dot_general | solution.py:263
  416.8 11.2 %multiply_convert_fusion.8 = bf16[8,512,1024]{2,1,0:T(8,128)(2,1)} fusion(f32[8,512,1024]{2,1,0:T(8,128)} %get-tuple-element.364, f32[8,512,1024]{2,1,0:T(8,128)S(1)} %copy-done.1, f32[8,512]{1,0:T(8,128)S(1)} %get-tuple-element.365, f32[8,512]{1,0:T(8,128)S(1)} %dynamic-slice_bitcast_fusion.2), kind=kLoop, calls=%fused_computation.13.clone.1 | loop fusion | flops 20971520 | bytes 41975808 | tf_op jit(solution)/shard_map/while/body/eval_jaxpr/convert_element_type | solution.py:267
  428.1 7.5 %fusion.164 = bf16[2,8,512,72]{2,3,1,0:T(8,128)(2,1)} fusion(bf16[2,8,512,72]{2,3,1,0:T(8,128)(2,1)} %get-tuple-element.401, s32[]{:T(128)S(6)} %copy.99, bf16[8,512,1024]{2,1,0:T(8,128)(2,1)} %multiply_convert_fusion.8, bf16[8,1024,72]{1,2,0:T(8,128)(2,1)} %copy-done.3), kind=kOutput, calls=%fused_computation.24.clone.1 | convolution fusion | flops 604274688 | bytes 10747908 | tf_op jit(solution)/shard_map/while/body/eval_jaxpr/hqk,hkd->hqd/dot_general | solution.py:269
  438.6 8.1 %fusion.163 = f32[8,512,1024]{2,1,0:T(8,128)} fusion(bf16[8,1024,72]{1,2,0:T(8,128)(2,1)S(1)} %get-tuple-element.414, bf16[2,8,512,72]{2,3,1,0:T(8,128)(2,1)S(1)} %get-tuple-element.413, s32[]{:T(128)S(6)} %copy.99), kind=kOutput, calls=%fused_computation.29.clone.1 | convolution fusion | flops 603979776 | bytes 18546692 | tf_op jit(solution)/shard_map/while/body/eval_jaxpr/hqd,hkd->hqk/dot_general | solution.py:259
  446.8 11.1 %select_add_fusion.5 = f32[8,1024,72]{1,2,0:T(8,128)} fusion(f32[8,1024,72]{1,2,0:T(8,128)} %get-tuple-element.400, f32[8,512,1024]{2,1,0:T(8,128)} %fusion.163, f32[8,512]{1,0:T(8,128)S(1)} %dynamic-slice_bitcast_fusion.2, pred[]{:T(512)S(6)} %compare.19, bf16[2,8,512,72]{2,3,1,0:T(8,128)(2,1)} %get-tuple-element.416, s32[]{:T(128)S(6)} %copy.99), kind=kOutput, calls=%fused_computation.20.clone.1 | convolution fusion | flops 617742336 | bytes 22102020 | tf_op jit(solution)/shard_map/while/body/eval_jaxpr/hqk,hqd->hkd/dot_general | solution.py:279
  457.9 14.6 %multiply_reduce_fusion.11 = (f32[8,512]{1,0:T(8,128)S(1)}, f32[8,512,1024]{2,1,0:T(8,128)}) fusion(f32[8,512,1024]{2,1,0:T(8,128)} %fusion.163, f32[8,512]{1,0:T(8,128)S(1)} %dynamic-slice_bitcast_fusion.2, bf16[8,1024,72]{1,2,0:T(8,128)(2,1)} %get-tuple-element.417, bf16[2,8,512,72]{2,3,1,0:T(8,128)(2,1)} %get-tuple-element.416, s32[]{:T(128)S(6)} %copy.99), kind=kOutput, calls=%fused_computation.14.clone.1 | convolution fusion | flops 620752896 | bytes 35356676 | tf_op jit(solution)/shard_map/while/body/eval_jaxpr/hqd,hkd->hqk/dot_general | solution.py:263
  475.0 10.4 %multiply_convert_fusion.8 = bf16[8,512,1024]{2,1,0:T(8,128)(2,1)} fusion(f32[8,512,1024]{2,1,0:T(8,128)} %get-tuple-element.364, f32[8,512,1024]{2,1,0:T(8,128)S(1)} %copy-done.1, f32[8,512]{1,0:T(8,128)S(1)} %get-tuple-element.365, f32[8,512]{1,0:T(8,128)S(1)} %dynamic-slice_bitcast_fusion.2), kind=kLoop, calls=%fused_computation.13.clone.1 | loop fusion | flops 20971520 | bytes 41975808 | tf_op jit(solution)/shard_map/while/body/eval_jaxpr/convert_element_type | solution.py:267
  485.4 7.4 %fusion.164 = bf16[2,8,512,72]{2,3,1,0:T(8,128)(2,1)} fusion(bf16[2,8,512,72]{2,3,1,0:T(8,128)(2,1)} %get-tuple-element.401, s32[]{:T(128)S(6)} %copy.99, bf16[8,512,1024]{2,1,0:T(8,128)(2,1)} %multiply_convert_fusion.8, bf16[8,1024,72]{1,2,0:T(8,128)(2,1)} %copy-done.3), kind=kOutput, calls=%fused_computation.24.clone.1 | convolution fusion | flops 604274688 | bytes 10747908 | tf_op jit(solution)/shard_map/while/body/eval_jaxpr/hqk,hkd->hqd/dot_general | solution.py:269
  492.8 4.8 select_add_fusion.4
  503.7 67.8 %reduce-scatter.11.cloned.1.call-done = bf16[72,2304]{1,0:T(8,128)(2,1)} async-done(((bf16[1152,2304]{1,0:T(8,128)(2,1)}), bf16[72,2304]{1,0:T(8,128)(2,1)}) %reduce-scatter.11.cloned.1.call-update) | async-done | bytes 331792 | tf_op jit(solution)/shard_map/reduce_scatter | solution.py:110
  571.5 7.6 %convolution_convert_fusion.2 = bf16[1152,3,576]{2,0,1:T(8,128)(2,1)S(1)} fusion(bf16[1024,3,576]{0,2,1:T(8,128)(2,1)} %pad_maximum_fusion, bf16[512,1152]{1,0:T(8,128)(2,1)S(1)} %copy-done.56, bf16[512,1152]{1,0:T(8,128)(2,1)S(1)} %copy-done.24), kind=kOutput, calls=%fused_computation.54 | convolution fusion | flops 4083572736 | bytes 9879552 | tf_op jit(solution)/shard_map/dot_general | solution.py:56
  579.1 18.2 %copy.56 = bf16[1152,3,576]{2,1,0:T(4,128)(2,1)} copy(bf16[1152,3,576]{2,0,1:T(8,128)(2,1)S(1)} %convolution_convert_fusion.2) | data formatting | bytes 7962624
  597.3 12.3 %reshape.225 = bf16[1152,1728]{1,0:T(8,128)(2,1)} reshape(bf16[1152,3,576]{2,1,0:T(4,128)(2,1)} %copy.56) | data formatting | bytes 7962624
  609.7 6.8 fusion.43
  621.8 21.3 %collective-permute-done.23 = bf16[512,1152]{1,0:T(8,128)(2,1)} collective-permute-done((bf16[512,1152]{1,0:T(8,128)(2,1)}, bf16[512,1152]{1,0:T(8,128)(2,1)}, u32[]{:S(2)}, u32[]{:S(2)}) %collective-permute-start.23) | collective-permute-done | bytes 1179680 | tf_op jit(solution)/shard_map/ppermute | solution.py:80
  643.1 6.9 %fusion.59 = (f32[1152]{0:T(1024)S(1)}, f32[512]{0:T(512)S(1)}, f32[512]{0:T(512)S(1)}, f32[1152]{0:T(1024)S(1)}, f32[512,1152]{1,0:T(8,128)S(1)}) fusion(bf16[1,512,1152]{2,1,0:T(8,128)(2,1)S(1)} %copy-done.13, f32[512]{0:T(512)S(1)} %copy-done.48, f32[512]{0:T(512)S(1)} %copy-done.44, f32[1152]{0:T(1024)S(1)} %copy-done.35, ...), kind=kOutput, calls=%fused_computation.87 | convolution fusion | flops 2045506304 | bytes 10933760 | tf_op jit(solution)/shard_map/dot_general | solution.py:62
  654.1 11.2 %all_to_all.30 = f32[16,1,1008]{2,1,0:T(1,128)S(1)} all-to-all(f32[16,1,1008]{2,1,0:T(1,128)S(1)} %all_to_all.22), channel_id=1, replica_groups=mesh['fsdp'=16,'tp'=2] {'fsdp'}, dimensions={0} | all-to-all | bytes 129024 | tf_op jit(solution)/shard_map/all_to_all | solution.py:121
  (328 shorter events, 147.1 us)
Async XLA Ops:
  7.2 58.2 %copy-start = (bf16[576,432]{0,1:T(8,128)(2,1)S(1)}, bf16[576,432]{0,1:T(8,128)(2,1)}, u32[]{:S(2)}) copy-start(bf16[576,432]{0,1:T(8,128)(2,1)} %param.19) | copy-start | bytes 1492996
  7.2 59.9 %copy-start.12 = (bf16[1,512,1152]{2,1,0:T(8,128)(2,1)S(1)}, bf16[1,512,1152]{2,1,0:T(8,128)(2,1)}, u32[]{:S(2)}) copy-start(bf16[1,512,1152]{2,1,0:T(8,128)(2,1)} %param.17) | copy-start | bytes 3538948
  7.2 76.7 %all-gather.5.cloned.1.call-start = ((), (), s32[]{:S(2)}) async-start(), calls=%async_computation.7 | async-start | bytes 4700160 | tf_op jit(solution)/shard_map/all_gather | solution.py:153
  7.9 59.6 %copy-start.52 = (bf16[432]{0:T(512)(128)(2,1)S(1)}, bf16[432]{0:T(512)(128)(2,1)}, u32[]{:S(2)}) copy-start(bf16[432]{0:T(512)(128)(2,1)} %param.20) | copy-start | bytes 2596
  8.0 145.0 %all-gather.7.cloned.1.call-start = ((), (), s32[]{:S(2)}) async-start(), calls=%async_computation.8 | async-start | bytes 1566720 | tf_op jit(solution)/shard_map/all_gather | solution.py:154
  8.7 211.3 %all-gather.9.cloned.1.call-start = ((), (), s32[]{:S(2)}) async-start(), calls=%async_computation.9 | async-start | bytes 5640192 | tf_op jit(solution)/shard_map/all_gather | solution.py:155
  13.0 7.2 %collective-permute-start.1 = (bf16[8,256]{1,0:T(8,128)(2,1)S(1)}, bf16[8,256]{1,0:T(8,128)(2,1)S(1)}, u32[]{:S(2)}, u32[]{:S(2)}) collective-permute-start(bf16[8,256]{1,0:T(8,128)(2,1)S(1)} %reshape.202), channel_id=1, source_target_pairs={{0,30},{2,0},{4,2},{6,4},{8,6},{10,8},{12,10},{14,12},{16,14},{18,... | collective-permute-start | bytes 12296 | tf_op jit(solution)/shard_map/ppermute | solution.py:32
  18.5 6.2 collective-permute-start
  20.1 61.8 %copy-start.43 = (f32[512]{0:T(512)}, f32[512]{0:T(512)S(1)}, u32[]{:S(2)}) copy-start(f32[512]{0:T(512)S(1)} %broadcast_multiply_fusion.5) | copy-start | bytes 6148
  20.2 5.8 collective-permute-start.3
  24.7 5.8 collective-permute-start.2
  26.1 5.8 collective-permute-start.5
  30.5 5.8 collective-permute-start.4
  31.8 5.7 collective-permute-start.7
  36.3 5.7 collective-permute-start.6
  37.6 5.7 collective-permute-start.9
  42.0 5.9 collective-permute-start.8
  43.3 5.9 collective-permute-start.11
  47.9 5.9 collective-permute-start.10
  49.2 10.3 %collective-permute-start.13 = (bf16[8,256]{1,0:T(8,128)(2,1)S(1)}, bf16[8,256]{1,0:T(8,128)(2,1)S(1)}, u32[]{:S(2)}, u32[]{:S(2)}) collective-permute-start(bf16[8,256]{1,0:T(8,128)(2,1)S(1)} %collective-permute-done.11), channel_id=1, source_target_pairs={{0,30},{2,0},{4,2},{6,4},{8,6},{10,8},{12,10},{14,12},{16,14},{18,... | collective-permute-start | bytes 12296 | tf_op jit(solution)/shard_map/ppermute | solution.py:32
  53.8 5.7 collective-permute-start.12
  59.5 5.7 collective-permute-start.14
  65.6 3.9 collective-permute-start.15
  70.2 10.3 %all-to-all-start = ((f32[16,1,432]{2,1,0:T(1,128)}), f32[16,1,432]{2,1,0:T(1,128)S(1)}, u32[]{:S(2)}, u32[]{:S(2)}) async-start(f32[16,1,432]{2,1,0:T(1,128)} %copy.43), calls=%async_computation | async-start | bytes 65536 | tf_op jit(solution)/shard_map/all_to_all | solution.py:121
  73.7 168.5 %all-gather.11.cloned.1.call-start = ((), (), s32[]{:S(2)}) async-start(), calls=%async_computation.10 | async-start | bytes 5640192 | tf_op jit(solution)/shard_map/all_gather | solution.py:156
  81.9 27.5 %collective-permute-start.16 = (bf16[512,1152]{1,0:T(8,128)(2,1)S(1)}, bf16[512,1152]{1,0:T(8,128)(2,1)S(1)}, u32[]{:S(2)}, u32[]{:S(2)}) collective-permute-start(bf16[512,1152]{1,0:T(8,128)(2,1)S(1)} %fusion.53), channel_id=1, source_target_pairs={{0,1},{1,0},{2,3},{3,2},{4,5},{5,4},{6,7},{7,6},{8,9},{9,8},{10,11... | collective-permute-start | bytes 3538952 | tf_op jit(solution)/shard_map/ppermute | solution.py:80
  83.4 420.3 %reduce-scatter.15.cloned.1.call-start = ((), (), s32[]{:S(2)}) async-start(), calls=%async_computation.14 | async-start | bytes 1566720
  152.9 30.9 %copy-start.33 = (f32[1152]{0:T(1024)S(1)}, f32[1152]{0:T(1024)}, u32[]{:S(2)}) copy-start(f32[1152]{0:T(1024)} %get-tuple-element.196) | copy-start | bytes 13828
  156.7 27.0 %collective-permute-start.17 = (bf16[512,1152]{1,0:T(8,128)(2,1)}, bf16[512,1152]{1,0:T(8,128)(2,1)}, u32[]{:S(2)}, u32[]{:S(2)}) collective-permute-start(bf16[512,1152]{1,0:T(8,128)(2,1)} %convolution_convert_fusion.6), channel_id=1, source_target_pairs={{0,1},{1,0},{2,3},{3,2},{4,5},{5,4},{6,7},{7,6},{8,9},{9,8},{10,11... | collective-permute-start | bytes 3538952 | tf_op jit(solution)/shard_map/ppermute | solution.py:80
  160.3 28.3 %copy-start.36 = (f32[1152]{0:T(1024)}, f32[1152]{0:T(1024)S(1)}, u32[]{:S(2)}) copy-start(f32[1152]{0:T(1024)S(1)} %add.374) | copy-start | bytes 13828
  190.8 29.2 %collective-permute-start.18 = (bf16[512,1152]{1,0:T(8,128)(2,1)}, bf16[512,1152]{1,0:T(8,128)(2,1)}, u32[]{:S(2)}, u32[]{:S(2)}) collective-permute-start(bf16[512,1152]{1,0:T(8,128)(2,1)} %add_convert_fusion.1), channel_id=1, source_target_pairs={{0,1},{1,0},{2,3},{3,2},{4,5},{5,4},{6,7},{7,6},{8,9},{9,8},{10,11... | collective-permute-start | bytes 3538952 | tf_op jit(solution)/shard_map/ppermute | solution.py:80
  196.5 45.7 %collective-permute-start.20 = (bf16[512,1152]{1,0:T(8,128)(2,1)}, bf16[512,1152]{1,0:T(8,128)(2,1)}, u32[]{:S(2)}, u32[]{:S(2)}) collective-permute-start(bf16[512,1152]{1,0:T(8,128)(2,1)} %get-tuple-element.232), channel_id=1, source_target_pairs={{0,1},{1,0},{2,3},{3,2},{4,5},{5,4},{6,7},{7,6},{8,9},{9,8},{10,11... | collective-permute-start | bytes 3538952 | tf_op jit(solution)/shard_map/ppermute | solution.py:80
  264.4 29.0 %collective-permute-start.21 = (bf16[512,1152]{1,0:T(8,128)(2,1)S(1)}, bf16[512,1152]{1,0:T(8,128)(2,1)S(1)}, u32[]{:S(2)}, u32[]{:S(2)}) collective-permute-start(bf16[512,1152]{1,0:T(8,128)(2,1)S(1)} %convolution_convert_fusion.4), channel_id=1, source_target_pairs={{0,1},{1,0},{2,3},{3,2},{4,5},{5,4},{6,7},{7,6},{8,9},{9,8},{10,11... | collective-permute-start | bytes 3538952 | tf_op jit(solution)/shard_map/ppermute | solution.py:80
  269.1 45.5 %collective-permute-start.19 = (bf16[512,1152]{1,0:T(8,128)(2,1)S(1)}, bf16[512,1152]{1,0:T(8,128)(2,1)S(1)}, u32[]{:S(2)}, u32[]{:S(2)}) collective-permute-start(bf16[512,1152]{1,0:T(8,128)(2,1)S(1)} %convolution_convert_fusion.5), channel_id=1, source_target_pairs={{0,1},{1,0},{2,3},{3,2},{4,5},{5,4},{6,7},{7,6},{8,9},{9,8},{10,11... | collective-permute-start | bytes 3538952 | tf_op jit(solution)/shard_map/ppermute | solution.py:80
  274.7 39.9 %copy-start.17 = (bf16[1,512,1152]{2,1,0:T(8,128)(2,1)S(1)}, bf16[1,512,1152]{2,1,0:T(8,128)(2,1)}, u32[]{:S(2)}) copy-start(bf16[1,512,1152]{2,1,0:T(8,128)(2,1)} %param.29) | copy-start | bytes 3538948
  314.6 29.1 %copy-start.19 = (bf16[2,8,9,8,512]{4,3,0,2,1:T(8,128)(2,1)S(1)}, bf16[2,8,9,8,512]{4,3,0,2,1:T(8,128)(2,1)}, u32[]{:S(2)}) copy-start(bf16[2,8,9,8,512]{4,3,0,2,1:T(8,128)(2,1)} %copy-done.18) | copy-start | bytes 3538948
  318.6 24.0 %collective-permute-start.22 = (bf16[512,1152]{1,0:T(8,128)(2,1)S(1)}, bf16[512,1152]{1,0:T(8,128)(2,1)S(1)}, u32[]{:S(2)}, u32[]{:S(2)}) collective-permute-start(bf16[512,1152]{1,0:T(8,128)(2,1)S(1)} %get-tuple-element.247), channel_id=1, source_target_pairs={{0,1},{1,0},{2,3},{3,2},{4,5},{5,4},{6,7},{7,6},{8,9},{9,8},{10,11... | collective-permute-start | bytes 3538952 | tf_op jit(solution)/shard_map/ppermute | solution.py:80
  346.9 156.7 %reduce-scatter.9.cloned.1.call-start = ((), (), s32[]{:S(2)}) async-start(), calls=%async_computation.11 | async-start | bytes 5640192 | tf_op jit(solution)/shard_map/reduce_scatter | solution.py:110
  357.9 213.5 %reduce-scatter.11.cloned.1.call-start = ((), (), s32[]{:S(2)}) async-start(), calls=%async_computation.12 | async-start | bytes 5640192 | tf_op jit(solution)/shard_map/reduce_scatter | solution.py:110
  368.6 313.2 %reduce-scatter.13.cloned.1.call-start = ((), (), s32[]{:S(2)}) async-start(), calls=%async_computation.13 | async-start | bytes 4386816
  501.3 70.1 %copy-start.24 = (bf16[512,1152]{1,0:T(8,128)(2,1)S(1)}, bf16[512,1152]{1,0:T(8,128)(2,1)}, u32[]{:S(2)}) copy-start(bf16[512,1152]{1,0:T(8,128)(2,1)} %copy-done.23) | copy-start | bytes 3538948
  501.3 70.1 %copy-start.56 = (bf16[512,1152]{1,0:T(8,128)(2,1)S(1)}, bf16[512,1152]{1,0:T(8,128)(2,1)}, u32[]{:S(2)}) copy-start(bf16[512,1152]{1,0:T(8,128)(2,1)} %copy-done.55) | copy-start | bytes 3538948
  616.4 26.7 %collective-permute-start.23 = (bf16[512,1152]{1,0:T(8,128)(2,1)}, bf16[512,1152]{1,0:T(8,128)(2,1)}, u32[]{:S(2)}, u32[]{:S(2)}) collective-permute-start(bf16[512,1152]{1,0:T(8,128)(2,1)} %fusion.43), channel_id=1, source_target_pairs={{0,1},{1,0},{2,3},{3,2},{4,5},{5,4},{6,7},{7,6},{8,9},{9,8},{10,11... | collective-permute-start | bytes 3538952 | tf_op jit(solution)/shard_map/ppermute | solution.py:80
  621.8 28.3 %copy-start.14 = (f32[512,1152]{1,0:T(8,128)S(1)}, f32[512,1152]{1,0:T(8,128)}, u32[]{:S(2)}) copy-start(f32[512,1152]{1,0:T(8,128)} %get-tuple-element.257) | copy-start | bytes 7077892
  621.8 28.3 %copy-start.16 = (f32[512,1152]{1,0:T(8,128)S(1)}, f32[512,1152]{1,0:T(8,128)}, u32[]{:S(2)}) copy-start(f32[512,1152]{1,0:T(8,128)} %get-tuple-element.248) | copy-start | bytes 7077892
  621.8 28.3 %copy-start.37 = (f32[1152]{0:T(1024)S(1)}, f32[1152]{0:T(1024)}, u32[]{:S(2)}) copy-start(f32[1152]{0:T(1024)} %copy-done.36) | copy-start | bytes 13828
  665.3 4.3 collective-permute-start.24
  670.7 10.4 %all-to-all-start.2 = ((f32[16,1,576]{2,1,0:T(1,128)}), f32[16,1,576]{2,1,0:T(1,128)S(1)}, u32[]{:S(2)}, u32[]{:S(2)}) async-start(f32[16,1,576]{2,1,0:T(1,128)} %copy.52), calls=%async_computation.4 | async-start | bytes 81920 | tf_op jit(solution)/shard_map/all_to_all | solution.py:121
  (55 other events, 544.6 us)
Sparse Core Ops, SparseCore 0:
  10.2 54.6 all-gather.4
  67.1 38.5 all-gather.6
  107.9 55.1 all-gather.8
  165.2 54.9 all-gather.10
  347.1 59.3 reduce-scatter.14
  410.3 78.4 reduce-scatter.8
  492.8 78.5 reduce-scatter.10
  609.7 71.9 reduce-scatter.12
